TPU v7x, 32 devices: a whole 2x2x4 slice. The times are simulated.
32 devices in a mesh: term: 2 (over x), sector: 16 (over z, y, core).
Axes of the slice: x: 2, y: 2, z: 4, core: 2. Of those that a mesh axis runs over, the one named last changes fastest.
Arguments:
- psi_start: bfloat16 [128, 256, 256], P('sector'), may hold values from -6 to 6
- left_env: bfloat16 [6, 128, 256, 256], P('term', 'sector')
- right_env: bfloat16 [6, 128, 256, 256], P('term', 'sector')
- connect: int32 [6, 128], P('term', 'sector'), may hold values from 0 to 127, as said below
- sector_dims: int32 [2, 128], P(None, 'sector'), may hold values from 64 to 256
- precond: bfloat16 [128, 256, 256], P('sector'), may hold values from 0.5 to 4
Outputs:
- projected: float32 [3, 3], replicated
- last_vector: float32 [128, 256, 256], P('sector', 'term')
- new_env: bfloat16 [6, 128, 256, 256], P('term', 'sector')
Inputs may be any that keep to these rules, and one draw needn't show every extreme that they name: connect[t, s] differs from s by at most 8.
All inputs are finite; a program needn't handle non-finite values.
Results may differ from a plain program's by a relative error of at most 0.012.
Values may be sent and summed in bfloat16 or wider, within the bound.
A program may use at most 128 MiB of HBM per device.

v0:
```python
import jax
import jax.numpy as jnp
from jax import lax
from jax.sharding import PartitionSpec as P

epsilon = 1e-06


def with_halo(block, sides, width):
    for axis, dim in sides:
        count = lax.axis_size(axis)
        forward = [(i, i + 1) for i in range(count - 1)]
        backward = [(target, source) for source, target in forward]
        low = lax.ppermute(
            lax.slice_in_dim(block, block.shape[dim] - width, None, axis=dim), axis, forward
        )
        high = lax.ppermute(lax.slice_in_dim(block, 0, width, axis=dim), axis, backward)
        block = jnp.concatenate([low, block, high], axis=dim)
    return block


def on_device(psi_start, left_env, right_env, connect, sector_dims, precond):
    blocks = psi_start.shape[0]
    width = psi_start.shape[1]
    devices = lax.axis_size("sector")
    pieces = lax.axis_size("term")
    terms_here = left_env.shape[0]
    entries = float(blocks * devices * width * width)
    local_source = connect - (lax.axis_index("sector") * blocks - blocks)
    share = width // pieces
    share_start = lax.axis_index("term") * share
    row_ids = lax.broadcasted_iota(jnp.int32, (blocks, width, width), 1)
    col_ids = lax.broadcasted_iota(jnp.int32, (blocks, width, width), 2)
    keep = (row_ids < sector_dims[0][:, None, None]) & (col_ids < sector_dims[1][:, None, None])
    mask = keep.astype(jnp.float32)
    start_rows = psi_start.astype(jnp.float32) * mask
    divisor = precond.astype(jnp.float32)

    def totals(values):
        stacked = jnp.stack(values)
        summed = lax.psum(stacked, "sector")
        return summed / entries

    norm_start = totals([jnp.sum(start_rows * start_rows)])[0]
    basis = [start_rows / jnp.sqrt(norm_start + epsilon)]
    sigmas = []
    env_list = []
    for which in range(3):
        vector_b = basis[which].astype(jnp.bfloat16)
        extended = with_halo(vector_b, (("sector", 0),), blocks)
        with_env = which == 2
        total = jnp.zeros((blocks, width, width), jnp.float32)
        own_blocks = extended[blocks : 2 * blocks]
        envs = []
        for apply_which in range(terms_here):
            source = jnp.take(extended, local_source[apply_which], axis=0)
            half = jnp.einsum(
                "sij,sjk->sik", left_env[apply_which], source, preferred_element_type=jnp.float32
            ).astype(jnp.bfloat16)
            total = total + jnp.einsum(
                "sik,slk->sil", half, right_env[apply_which], preferred_element_type=jnp.float32
            )
            if with_env:
                env_one = jnp.einsum(
                    "sji,sjk->sik", own_blocks, half, preferred_element_type=jnp.float32
                ) * width ** (-0.5)
                envs.append(env_one.astype(jnp.bfloat16))
        sigma = lax.psum(total, "term")
        sigma, env_list = (sigma * mask, envs)
        sigmas.append(sigma)
        if which < 2:
            theta = totals([jnp.sum(basis[which] * sigma)])[0]
            corr = (sigma - theta * basis[which]) / divisor
            correlations = totals([jnp.sum(member * corr) for member in basis])
            for position in range(len(basis)):
                corr = corr - correlations[position] * basis[position]
            length = totals([jnp.sum(corr * corr)])[0]
            basis.append(corr / jnp.sqrt(length + epsilon))
    products = totals([jnp.sum(basis[row] * sigmas[col]) for row in range(3) for col in range(3)])
    projected = products.reshape(3, 3)
    last_vector = lax.dynamic_slice_in_dim(basis[2], share_start, share, 1)
    return (projected, last_vector, jnp.stack(env_list))


def solution(mesh):
    placed = (
        P("sector", None, None),
        P("term", "sector", None, None),
        P("term", "sector", None, None),
        P("term", "sector"),
        P(None, "sector"),
        P("sector", None, None),
    )
    return jax.shard_map(
        on_device,
        mesh=mesh,
        in_specs=placed,
        out_specs=(P(), P("sector", "term", None), P("term", "sector", None, None)),
        check_vma=False,
    )
```

profile of v0, /device:TPU:0, one launch (start us, length us, event | category | flops | bytes accessed | tf_op | source)
XLA Modules:
  0.0 646.5 jit_solution(17308843335064194327)
XLA Ops:
  8.0 2.4 multiply_reduce_fusion.14
  10.4 35.6 %psum.77 = f32[1]{0:T(128)} all-reduce(f32[1]{0:T(128)} %bitcast.2), channel_id=1, replica_groups=mesh['term'=2,'sector'=16] {'sector'}, use_global_device_ids=true, to_apply=%region_1.0 | all-reduce | flops 1 | bytes 8 | tf_op jit(solution)/shard_map/psum | solution.py:41
  46.7 1.8 fusion.119
  54.5 2.0 pad_maximum_fusion
  59.7 1.6 gather_fusion.2
  61.3 4.2 fusion.3
  65.5 3.7 fusion.2
  69.2 5.0 add_add_fusion.2
  74.3 79.1 %all-reduce.4.cloned.1.call-done = f32[8,256,256]{2,1,0:T(8,128)} async-done(((f32[8,256,256]{2,1,0:T(8,128)}), f32[8,256,256]{2,1,0:T(8,128)}) %all-reduce.4.cloned.1.call-update) | async-done | bytes 2097168 | tf_op jit(solution)/shard_map/psum | solution.py:68
  153.4 3.0 multiply_reduce_fusion.13
  156.5 33.6 %psum.79 = f32[1]{0:T(128)} all-reduce(f32[1]{0:T(128)} %bitcast.13), channel_id=1, replica_groups=mesh['term'=2,'sector'=16] {'sector'}, use_global_device_ids=true, to_apply=%region_4.6 | all-reduce | flops 1 | bytes 8 | tf_op jit(solution)/shard_map/psum | solution.py:41
  190.8 2.8 multiply_reduce_fusion.12
  193.6 30.1 %psum.80 = f32[1]{0:T(128)} all-reduce(f32[1]{0:T(128)} %bitcast.15), channel_id=1, replica_groups=mesh['term'=2,'sector'=16] {'sector'}, use_global_device_ids=true, to_apply=%region_6.8 | all-reduce | flops 1 | bytes 8 | tf_op jit(solution)/shard_map/psum | solution.py:41
  224.3 3.6 multiply_reduce_fusion.11
  227.9 30.1 %psum.81 = f32[1]{0:T(128)} all-reduce(f32[1]{0:T(128)} %bitcast.17), channel_id=1, replica_groups=mesh['term'=2,'sector'=16] {'sector'}, use_global_device_ids=true, to_apply=%region_8.10 | all-reduce | flops 1 | bytes 8 | tf_op jit(solution)/shard_map/psum | solution.py:41
  258.9 1.8 collective-permute-start.2
  263.0 2.4 collective-permute-done.3
  265.3 1.8 pad_maximum_fusion.1
  267.2 3.5 gather_fusion.4
  270.6 3.5 gather_fusion.3
  274.1 3.5 gather_fusion.5
  277.6 4.0 fusion.5
  281.6 4.0 fusion.4
  285.6 5.3 add_add_fusion.1
  291.2 79.4 %all-reduce.6.cloned.1.call-done = f32[8,256,256]{2,1,0:T(8,128)} async-done(((f32[8,256,256]{2,1,0:T(8,128)}), f32[8,256,256]{2,1,0:T(8,128)}) %all-reduce.6.cloned.1.call-update) | async-done | bytes 2097168 | tf_op jit(solution)/shard_map/psum | solution.py:68
  370.5 2.9 multiply_reduce_fusion.9
  373.4 33.6 %psum.83 = f32[1]{0:T(128)} all-reduce(f32[1]{0:T(128)} %bitcast.20), channel_id=1, replica_groups=mesh['term'=2,'sector'=16] {'sector'}, use_global_device_ids=true, to_apply=%region_12.14 | all-reduce | flops 1 | bytes 8 | tf_op jit(solution)/shard_map/psum | solution.py:41
  407.7 3.9 multiply_reduce_fusion.8
  413.0 29.5 %psum.84 = f32[2]{0:T(128)S(1)} all-reduce(f32[2]{0:T(128)S(1)} %pad_maximum_fusion.4), channel_id=1, replica_groups=mesh['term'=2,'sector'=16] {'sector'}, use_global_device_ids=true, to_apply=%region_15.17 | all-reduce | flops 2 | bytes 16 | tf_op jit(solution)/shard_map/psum | solution.py:41
  443.1 6.4 multiply_reduce_fusion.6
  449.5 30.1 %psum.85 = f32[1]{0:T(128)} all-reduce(f32[1]{0:T(128)} %bitcast.26), channel_id=1, replica_groups=mesh['term'=2,'sector'=16] {'sector'}, use_global_device_ids=true, to_apply=%region_17.19 | all-reduce | flops 1 | bytes 8 | tf_op jit(solution)/shard_map/psum | solution.py:41
  480.3 3.2 fusion.121
  483.5 1.8 collective-permute-start.4
  487.5 2.4 collective-permute-done.5
  489.9 1.8 pad_maximum_fusion.2
  491.7 3.5 gather_fusion.6
  495.2 3.5 gather_fusion.7
  498.7 3.5 gather_fusion.8
  502.2 2.3 convolution_convert_fusion.8
  504.7 2.2 convolution_convert_fusion.7
  507.5 1.7 copy-done.5
  510.2 1.9 add_add_fusion
  512.2 2.4 constant_dynamic-slice_fusion
  519.2 72.6 %all-reduce.8.cloned.1.call-done = f32[8,256,256]{2,1,0:T(8,128)} async-done(((f32[8,256,256]{2,1,0:T(8,128)}), f32[8,256,256]{2,1,0:T(8,128)}) %all-reduce.8.cloned.1.call-update) | async-done | bytes 2097168 | tf_op jit(solution)/shard_map/psum | solution.py:68
  591.7 4.9 multiply_reduce_fusion
  596.6 5.8 stack.81
  602.4 3.9 pad_maximum_fusion.3
  606.3 33.0 %psum.87 = f32[9]{0:T(128)S(1)} all-reduce(f32[9]{0:T(128)S(1)} %stack.81), channel_id=1, replica_groups=mesh['term'=2,'sector'=16] {'sector'}, use_global_device_ids=true, to_apply=%region_25.27 | all-reduce | flops 9 | bytes 72 | tf_op jit(solution)/shard_map/psum | solution.py:41
  (66 shorter events, 23.9 us)
Async XLA Ops:
  7.2 44.0 %copy-start.16 = (s32[3,8]{1,0:T(4,128)S(1)}, s32[3,8]{1,0:T(4,128)}, u32[]{:S(2)}) copy-start(s32[3,8]{1,0:T(4,128)} %param.11) | copy-start | bytes 292
  7.2 146.2 %all-reduce.4.cloned.1.call-start = ((), (), s32[]{:S(2)}) async-start(), calls=%async_computation | async-start | bytes 4194304 | tf_op jit(solution)/shard_map/psum | solution.py:68
  48.5 3.6 copy-start.10
  48.5 3.6 collective-permute-start
  49.9 4.7 collective-permute-start.1
  52.1 1.0 copy-start.15
  61.3 4.2 copy-start.4
  74.2 79.2 %copy-start = (bf16[8,256,256]{2,1,0:T(8,128)(2,1)S(1)}, bf16[8,256,256]{2,1,0:T(8,128)(2,1)}, u32[]{:S(2)}) copy-start(bf16[8,256,256]{2,1,0:T(8,128)(2,1)} %param.8) | copy-start | bytes 3145732
  74.2 296.3 %all-reduce.6.cloned.1.call-start = ((), (), s32[]{:S(2)}) async-start(), calls=%async_computation.1 | async-start | bytes 4194304 | tf_op jit(solution)/shard_map/psum | solution.py:68
  153.4 37.3 %copy-start.1 = (f32[8,256,256]{2,1,0:T(8,128)S(1)}, f32[8,256,256]{2,1,0:T(8,128)}, u32[]{:S(2)}) copy-start(f32[8,256,256]{2,1,0:T(8,128)} %all-reduce.4.cloned.1.call-done) | copy-start | bytes 6291460
  258.9 4.0 collective-permute-start.2
  260.8 4.6 collective-permute-start.3
  290.9 300.8 %all-reduce.8.cloned.1.call-start = ((), (), s32[]{:S(2)}) async-start(), calls=%async_computation.2 | async-start | bytes 4194304 | tf_op jit(solution)/shard_map/psum | solution.py:68
  483.5 6.4 copy-start.2
  483.5 4.0 collective-permute-start.4
  485.3 4.6 collective-permute-start.5
  502.2 2.5 copy-start.13
  504.7 5.0 copy-start.6
  504.7 2.2 copy-start.14
  506.9 2.8 copy-start.8
  506.9 2.3 copy-start.5
  509.2 1.0 copy-start.11
  512.1 2.4 copy-start.3
  512.2 2.4 copy-start.7
  514.6 1.6 copy-start.9
  516.2 1.5 copy-start.12
Sparse Core Ops, SparseCore 0:
  74.4 79.0 all-reduce.3
  291.0 79.4 all-reduce.5
  512.3 79.4 all-reduce.7
where the time goes:
time: 648 us; the launch traced here: 646 us
  blocking collectives  256 us (40%)
  waiting for transfers between devices  240 us (37%)
  other arithmetic  46.1 us (7%)
  local copies, waits for them, and re-layouts  38.9 us (6%)
  matrix products  38.6 us (6%)
  between operations  18 us (3%)
  starting transfers between devices  9.19 us (1%)
    psum x8, blocking collectives, totals(): summed = lax.psum(stacked, 'sector')  256 us
    psum x3, waiting for transfers between devices, on_device(): sigma = lax.psum(total, 'term')  231 us
    dot_general x9, matrix products, on_device(): jnp.einsum('sik,slk->sil', half, right_env[apply_which], preferred_elemen...  29 us
    gather x9, local copies, waits for them, and re-layouts, on_device(): source = jnp.take(extended, local_source[apply_which], axis=0)  25.7 us
  transfers between devices with their start and end apart: 9, of which 9 were waited for; matrix products, arithmetic and copies ran while one was open for 1% of the time, Pallas kernels for 0%

commit v1 on v0

v1 whole, which is shorter than its diff:
```python
import functools
import jax
import jax.numpy as jnp
from jax import lax
from jax.experimental import pallas as pl
from jax.experimental.pallas import tpu as pltpu
from jax.sharding import PartitionSpec as P

epsilon = 1e-06
MESH = pl.DeviceIdType.MESH
F32 = jnp.float32
BF16 = jnp.bfloat16
ROWS = 16


def fold(values):
    rows, width = values.shape
    total = values.reshape(rows // 8, 8, width).sum(axis=0)
    out = total[:, :128]
    for start in range(128, width, 128):
        out = out + total[:, start : start + 128]
    return out


def kernel(
    sizes,
    dims, conn, psi, left, right, pre,
    proj, last, env,
    raw, ext1, ext2, ext3, acc, stage, came, sig1, sig2, base1, base2, tile, slots,
    halo_send, halo_recv, share_send, share_recv, part_send, part_recv, sum_send, sum_recv,
):
    pieces, devices, terms, blocks, width, entries = sizes
    share = width // pieces
    count = pieces * devices
    step = min(32, share)
    steps = share // step
    me_t = lax.axis_index("term")
    me_s = lax.axis_index("sector")
    me = me_t * devices + me_s
    first = me_s * blocks - blocks
    has_low = me_s > 0
    has_high = me_s < devices - 1
    zero = jnp.zeros((8, 128), F32)

    def device_at(offset):
        other = lax.rem(me + offset, count)
        return (other // devices, lax.rem(other, devices))

    def term_at(offset):
        return lax.rem(me_t + offset, pieces)

    def rows_of(piece):
        return pl.ds(pl.multiple_of(piece * share, share), share)

    barrier = pltpu.get_barrier_semaphore()

    @pl.loop(1, count)
    def _(offset):
        pl.semaphore_signal(barrier, inc=1, device_id=device_at(offset), device_id_type=MESH)

    pl.semaphore_wait(barrier, count - 1)

    def halo_copy(ref, s, j, up, rows):
        slot = s if up else 2 * blocks + s
        direction = 0 if up else 1
        return pltpu.make_async_remote_copy(
            src_ref=ref.at[blocks + s, rows],
            dst_ref=ref.at[slot, rows],
            send_sem=halo_send.at[direction, j, s],
            recv_sem=halo_recv.at[direction, j, s],
            device_id=(me_t, me_s + 1 if up else me_s - 1),
            device_id_type=MESH,
        )

    def halo_start(ref, s, j, rows):
        @pl.when(has_high)
        def _():
            halo_copy(ref, s, j, True, rows).start()

        @pl.when(has_low)
        def _():
            halo_copy(ref, s, j, False, rows).start()

    def halo_wait(ref, s, j, rows):
        @pl.when(has_high)
        def _():
            halo_copy(ref, s, j, True, rows).wait_send()
            halo_copy(ref, s, j, False, rows).wait_recv()

        @pl.when(has_low)
        def _():
            halo_copy(ref, s, j, False, rows).wait_send()
            halo_copy(ref, s, j, True, rows).wait_recv()

    def share_copy(ref, s, offset, piece):
        return pltpu.make_async_remote_copy(
            src_ref=ref.at[blocks + s, rows_of(piece)],
            dst_ref=ref.at[blocks + s, rows_of(piece)],
            send_sem=share_send.at[offset - 1, s],
            recv_sem=share_recv.at[offset - 1, s],
            device_id=(term_at(offset), me_s),
            device_id_type=MESH,
        )

    def part_copy(s, offset):
        return pltpu.make_async_remote_copy(
            src_ref=stage.at[offset - 1, s],
            dst_ref=came.at[offset - 1, s],
            send_sem=part_send.at[offset - 1, s],
            recv_sem=part_recv.at[offset - 1, s],
            device_id=(term_at(offset), me_s),
            device_id_type=MESH,
        )

    def sum_start(which, tiles):
        rows = [jnp.sum(one, axis=0, keepdims=True) for one in tiles]
        rows = rows + [jnp.zeros((1, 128), F32)] * (ROWS - len(rows))
        packed = jnp.concatenate(rows, axis=0)
        tile[which] = packed
        slots[which, me] = packed

        @pl.loop(1, count)
        def _(offset):
            pltpu.make_async_remote_copy(
                src_ref=tile.at[which],
                dst_ref=slots.at[which, me],
                send_sem=sum_send.at[which],
                recv_sem=sum_recv.at[which],
                device_id=device_at(offset),
                device_id_type=MESH,
            ).start()

    def sum_finish(which):
        others = slots.at[which, pl.ds(0, count - 1)]
        pltpu.make_async_copy(others, others, sum_recv.at[which]).wait()
        pltpu.make_async_copy(others, others, sum_send.at[which]).wait()
        total = lax.fori_loop(
            0, count, lambda i, t: t + slots[which, i], jnp.zeros((ROWS, 128), F32)
        )
        full = jnp.sum(total, axis=1, keepdims=True) / entries
        return lambda row: full[row : row + 1, :]

    row_ids = lax.broadcasted_iota(jnp.int32, (width, width), 0)
    col_ids = lax.broadcasted_iota(jnp.int32, (width, width), 1)
    all_rows = pl.ds(0, width)

    @pl.loop(0, blocks)
    def _(s):
        keep = (row_ids < dims[0, s]) & (col_ids < dims[1, s])
        raw[blocks + s] = jnp.where(keep, psi[s].astype(F32), 0.0).astype(BF16)
        halo_start(raw, s, 0, all_rows)

    def chunk(i):
        return i // steps, pl.multiple_of(lax.rem(i, steps) * step, step)

    def own_rows(start):
        return pl.ds(pl.multiple_of(me_t * share + start, step), step)

    def norm_step(i, total):
        s, start = chunk(i)
        v = raw[blocks + s, own_rows(start), :].astype(F32)
        return total + fold(v * v)

    sum_start(0, [lax.fori_loop(0, blocks * steps, norm_step, zero)])
    norm = sum_finish(0)(0)
    scale = 1.0 / jnp.sqrt(norm + epsilon)

    def scaled(slot):
        ext1[slot] = (raw[slot].astype(F32) * scale).astype(BF16)

    @pl.loop(0, blocks)
    def _(s):
        scaled(blocks + s)
        base1[s] = raw[blocks + s, rows_of(me_t), :].astype(F32) * scale

    @pl.loop(0, blocks)
    def _(s):
        halo_wait(raw, s, 0, all_rows)

        @pl.when(has_low)
        def _():
            scaled(s)

        @pl.when(has_high)
        def _():
            scaled(2 * blocks + s)

    def product(ref, s, with_env):
        halves = []
        for t in range(terms):
            source = ref[jnp.clip(conn[t, s] - first, 0, 3 * blocks - 1)]
            half = jnp.dot(left[t, s], source, preferred_element_type=F32).astype(BF16)
            halves.append(half)
        total = None
        for t in range(terms):
            one = lax.dot_general(
                halves[t], right[t, s], (((1,), (1,)), ((), ())), preferred_element_type=F32
            )
            total = one if total is None else total + one
            if with_env:
                new = lax.dot_general(
                    ref[blocks + s], halves[t], (((0,), (0,)), ((), ())),
                    preferred_element_type=F32,
                )
                env[t, s] = (new * width ** (-0.5)).astype(BF16)
        return total

    def apply(ref):
        @pl.loop(0, blocks)
        def _(s):
            acc[s] = product(ref, s, False)
            for offset in range(1, pieces):
                stage[offset - 1, s] = acc[s, rows_of(term_at(offset)), :].astype(BF16)
                part_copy(s, offset).start()

    def masked_sum(s, start):
        total = acc[s, own_rows(start), :]
        for offset in range(1, pieces):
            total = total + came[offset - 1, s, pl.ds(start, step), :].astype(F32)
        rows = lax.broadcasted_iota(jnp.int32, (step, width), 0) + (me_t * share + start)
        cols = lax.broadcasted_iota(jnp.int32, (step, width), 1)
        return jnp.where((rows < dims[0, s]) & (cols < dims[1, s]), total, 0.0)

    def divided(s, start):
        return 1.0 / pre[s, own_rows(start), :].astype(F32)

    def part_wait(s):
        for offset in range(1, pieces):
            part_copy(s, offset).wait()

    def spread(ref, out, corr_of, meanwhile=None):
        @pl.loop(0, blocks)
        def _(s):
            @pl.loop(0, steps)
            def _(k):
                start = pl.multiple_of(k * step, step)
                value = corr_of(s, start)
                out[s, pl.ds(start, step), :] = value
                ref[blocks + s, own_rows(start), :] = value.astype(BF16)

            for offset in range(1, pieces):
                share_copy(ref, s, offset, me_t).start()
            halo_start(ref, s, 0, rows_of(me_t))

        @pl.loop(0, blocks)
        def _(s):
            for offset in range(1, pieces):
                share_copy(ref, s, offset, term_at(pieces - offset)).wait_recv()
                halo_start(ref, s, offset, rows_of(term_at(pieces - offset)))

        extra = meanwhile() if meanwhile is not None else None

        @pl.loop(0, blocks)
        def _(s):
            for offset in range(1, pieces):
                share_copy(ref, s, offset, me_t).wait_send()
            for j in range(pieces):
                halo_wait(ref, s, j, rows_of(term_at(pieces - j)))
        return extra

    apply(ext1)

    def sums1(i, totals):
        s, start = chunk(i)
        here = pl.ds(start, step)

        @pl.when(start == 0)
        def _():
            part_wait(s)

        sigma = masked_sum(s, start)
        sig1[s, here, :] = sigma
        inverse = divided(s, start)
        b1 = base1[s, here, :]
        r = sigma * inverse
        q = b1 * inverse
        pairs = [(b1, sigma), (b1, r), (b1, q), (r, r), (r, q), (q, q), (b1, b1)]
        return tuple(t + fold(x * y) for t, (x, y) in zip(totals, pairs))

    sum_start(1, lax.fori_loop(0, blocks * steps, sums1, (zero,) * 7))
    got = sum_finish(1)
    theta1 = got(0)
    first_gram = got(6)
    weight = got(1) - theta1 * got(2)
    length = (
        (got(3) - 2.0 * theta1 * got(4) + theta1 * theta1 * got(5))
        - 2.0 * weight * weight
        + weight * weight * first_gram
    )
    scale1 = 1.0 / jnp.sqrt(jnp.maximum(length, 0.0) + epsilon)

    def corr1(s, start):
        here = pl.ds(start, step)
        b1 = base1[s, here, :]
        corr = (sig1[s, here, :] - theta1 * b1) * divided(s, start)
        return (corr - weight * b1) * scale1

    spread(ext2, base2, corr1)

    apply(ext2)

    def sums2(i, totals):
        s, start = chunk(i)
        here = pl.ds(start, step)

        @pl.when(start == 0)
        def _():
            part_wait(s)

        sigma = masked_sum(s, start)
        sig2[s, here, :] = sigma
        inverse = divided(s, start)
        b1 = base1[s, here, :]
        b2 = base2[s, here, :]
        r = sigma * inverse
        q = b2 * inverse
        pairs = [
            (b2, sigma), (b1, r), (b2, r), (b1, q), (b2, q), (r, r), (r, q), (q, q),
            (b1, b2), (b2, b2), (b1, sigma), (b2, sig1[s, here, :]),
        ]
        return tuple(t + fold(x * y) for t, (x, y) in zip(totals, pairs))

    sum_start(2, lax.fori_loop(0, blocks * steps, sums2, (zero,) * 12))
    more = sum_finish(2)
    theta2 = more(0)
    weight1 = more(1) - theta2 * more(3)
    weight2 = more(2) - theta2 * more(4)
    length2 = (
        (more(5) - 2.0 * theta2 * more(6) + theta2 * theta2 * more(7))
        - 2.0 * (weight1 * weight1 + weight2 * weight2)
        + weight1 * weight1 * first_gram
        + 2.0 * weight1 * weight2 * more(8)
        + weight2 * weight2 * more(9)
    )
    scale2 = 1.0 / jnp.sqrt(jnp.maximum(length2, 0.0) + epsilon)

    def corr2(s, start):
        here = pl.ds(start, step)
        b1 = base1[s, here, :]
        b2 = base2[s, here, :]
        corr = (sig2[s, here, :] - theta2 * b2) * divided(s, start)
        return (corr - weight1 * b1 - weight2 * b2) * scale2

    def cross(i, totals):
        s, start = chunk(i)
        here = pl.ds(start, step)
        b3 = last[s, here, :]
        pairs = [(b3, sig1[s, here, :]), (b3, sig2[s, here, :])]
        return tuple(t + fold(x * y) for t, (x, y) in zip(totals, pairs))

    crossed = spread(
        ext3, last, corr2, lambda: lax.fori_loop(0, blocks * steps, cross, (zero,) * 2)
    )

    def sums3(s, totals):
        acc[s] = product(ext3, s, True)

        def inner(k, totals):
            here = pl.ds(pl.multiple_of(k * step, step), step)
            sigma = acc[s, here, :]
            vectors = [ref[blocks + s, here, :].astype(F32) for ref in (ext1, ext2, ext3)]
            return tuple(t + fold(v * sigma) for t, v in zip(totals, vectors))

        return lax.fori_loop(0, width // step, inner, totals)

    sum_start(3, list(lax.fori_loop(0, blocks, sums3, (zero,) * 3)) + list(crossed))
    end = sum_finish(3)
    cells = [
        [theta1, more(10), end(0)],
        [more(11), theta2, end(1)],
        [end(3), end(4), end(2)],
    ]
    row = lax.broadcasted_iota(jnp.int32, (8, 128), 0)
    col = lax.broadcasted_iota(jnp.int32, (8, 128), 1)
    out = zero
    for i in range(3):
        for j in range(3):
            out = jnp.where((row == i) & (col == j), cells[i][j], out)
    proj[...] = out


def on_device(psi, left, right, connect, sector_dims, precond):
    blocks, width = psi.shape[0], psi.shape[1]
    terms = left.shape[0]
    pieces, devices = lax.axis_size("term"), lax.axis_size("sector")
    count = pieces * devices
    share = width // pieces
    entries = float(blocks * devices * width * width)
    sizes = (pieces, devices, terms, blocks, width, entries)
    others = max(pieces - 1, 1)
    dma = pltpu.SemaphoreType.DMA
    vmem = pl.BlockSpec(memory_space=pltpu.VMEM)
    smem = pl.BlockSpec(memory_space=pltpu.SMEM)
    proj, last, env = pl.pallas_call(
        functools.partial(kernel, sizes),
        name="davidson",
        out_shape=(
            jax.ShapeDtypeStruct((8, 128), F32),
            jax.ShapeDtypeStruct((blocks, share, width), F32),
            jax.ShapeDtypeStruct((terms, blocks, width, width), BF16),
        ),
        in_specs=[smem, smem, vmem, vmem, vmem, vmem],
        out_specs=(vmem, vmem, vmem),
        scratch_shapes=[
            pltpu.VMEM((3 * blocks, width, width), BF16),
            pltpu.VMEM((3 * blocks, width, width), BF16),
            pltpu.VMEM((3 * blocks, width, width), BF16),
            pltpu.VMEM((3 * blocks, width, width), BF16),
            pltpu.VMEM((blocks, width, width), F32),
            pltpu.VMEM((others, blocks, share, width), BF16),
            pltpu.VMEM((others, blocks, share, width), BF16),
            pltpu.VMEM((blocks, share, width), F32),
            pltpu.VMEM((blocks, share, width), F32),
            pltpu.VMEM((blocks, share, width), F32),
            pltpu.VMEM((blocks, share, width), F32),
            pltpu.VMEM((4, ROWS, 128), F32),
            pltpu.VMEM((4, count, ROWS, 128), F32),
            dma((2, pieces, blocks)),
            dma((2, pieces, blocks)),
            dma((others, blocks)),
            dma((others, blocks)),
            dma((others, blocks)),
            dma((others, blocks)),
            dma((4,)),
            dma((4,)),
        ],
        compiler_params=pltpu.CompilerParams(
            collective_id=0, has_side_effects=True, vmem_limit_bytes=60 * 1024 * 1024
        ),
    )(sector_dims, connect, psi, left, right, precond)
    return proj[:3, :3], last, env


def solution(mesh):
    placed = (
        P("sector", None, None),
        P("term", "sector", None, None),
        P("term", "sector", None, None),
        P("term", "sector"),
        P(None, "sector"),
        P("sector", None, None),
    )
    return jax.shard_map(
        on_device,
        mesh=mesh,
        in_specs=placed,
        out_specs=(P(), P("sector", "term", None), P("term", "sector", None, None)),
        check_vma=False,
    )
```

time: 648 us -> 147 us (0.23)
  blocking collectives: 256 us -> 0 us
  waiting for transfers between devices: 240 us -> 0 us
  Pallas kernels: 0 us -> 139 us
  other arithmetic: 46.1 us -> 0 us
  matrix products: 38.6 us -> 0 us
  local copies, waits for them, and re-layouts: 38.9 us -> 7.38 us
  between operations: 18 us -> 0.64 us
  starting transfers between devices: 9.19 us -> 0 us
    psum x8 -> x0, blocking collectives: 256 us -> none  [totals(): summed = lax.psum(stacked, 'sector')]
    psum x3 -> x0, waiting for transfers between devices: 231 us -> none  [on_device(): sigma = lax.psum(total, 'term')]
    pallas_call x0 -> x1, Pallas kernels: none -> 139 us  [on_device(): pl.pallas_call(functools.partial(kernel, sizes), name='davidson', out_sha...]
    dot_general x15 -> x0, matrix products: 38.6 us -> none  [the longest x9 29 us: on_device(): jnp.einsum('sik,slk->sil', half, right_env[apply_which], preferred_elemen...]
    reduce_sum x8 -> x0, other arithmetic: 30 us -> none  [the longest x2 10.1 us: on_device(): length = totals([jnp.sum(corr * corr)])[0]]
    gather x9 -> x0, local copies, waits for them, and re-layouts: 25.7 us -> none  [on_device(): source = jnp.take(extended, local_source[apply_which], axis=0)]
    ppermute x6 -> x0, starting transfers between devices: 8.89 us -> none  [the longest x3 5.01 us: with_halo(): lax.ppermute(lax.slice_in_dim(block, block.shape[dim] - width, None, axis...]
    ppermute x6 -> x0, waiting for transfers between devices: 8.85 us -> none  [the longest x3 6.21 us: with_halo(): lax.ppermute(lax.slice_in_dim(block, 0, width, axis=dim), axis, backward)]
  transfers between devices with their start and end apart: 9 -> 0, of which waited for: 9 -> 0; matrix products, arithmetic and copies ran while one was open for 1% -> 0% of each run, Pallas kernels for 0% -> 0%
where the time goes in v1:
time: 147 us
  Pallas kernels  139 us (95%)
  local copies, waits for them, and re-layouts  7.38 us (5%)
    pallas_call x1, Pallas kernels, on_device(): pl.pallas_call(functools.partial(kernel, sizes), name='davidson', out_sha...  139 us
    unnamed x2, local copies, waits for them, and re-layouts  6.12 us

profile of v1, /device:TPU:0, one launch (start us, length us, event | category | flops | bytes accessed | tf_op | source)
XLA Modules:
  0.0 146.7 jit_solution(7718782839855545036)
XLA Ops:
  0.6 138.6 %davidson.1 = (f32[8,128]{1,0:T(8,128)}, f32[8,128,256]{2,1,0:T(8,128)}, bf16[3,8,256,256]{3,2,1,0:T(8,128)(2,1)}) custom-call(s32[2,8]{1,0:T(2,128)} %dims.1, s32[3,8]{1,0:T(4,128)} %conn.1, bf16[8,256,256]{2,1,0:T(8,128)(2,1)} %psi.1, bf16[3,8,256,256]{3,2,1,0:T(8,128)(2,1)} %left.1, bf16[3,8,256,256]{3,2,1,0:T(8,128)(2,1)} %right.1, bf16[8,256,256]{2,1,0:T(8,128)(2,1)} %pre.1), custom_call_target="tpu_custom_call" | custom-call | tf_op jit(solution)/shard_map/davidson/pallas_call | solution.py:394
  139.3 1.3 slice.3
  140.5 2.3 %copy.11 = f32[8,128,256]{2,1,0:T(8,128)} copy(f32[8,128,256]{2,1,0:T(8,128)} %get-tuple-element.13) | data formatting | bytes 2097152
  142.8 3.9 %copy.12 = bf16[3,8,256,256]{3,2,1,0:T(8,128)(2,1)} copy(bf16[3,8,256,256]{3,2,1,0:T(8,128)(2,1)} %get-tuple-element.14) | data formatting | bytes 6291456

commit v2 on v1

--- a/solution.py
+++ b/solution.py
@@ -10,7 +10,6 @@
 MESH = pl.DeviceIdType.MESH
 F32 = jnp.float32
 BF16 = jnp.bfloat16
-ROWS = 16
 
 
 def fold(values):
@@ -24,10 +23,10 @@
 
 def kernel(
     sizes,
-    dims, conn, psi, left, right, pre,
-    proj, last, env,
-    raw, ext1, ext2, ext3, acc, stage, came, sig1, sig2, base1, base2, tile, slots,
-    halo_send, halo_recv, share_send, share_recv, part_send, part_recv, sum_send, sum_recv,
+    dims, conn, psi, left_in, right_in, pre_in,
+    proj, last, env_out,
+    left, right, pre, env, raw, ext1, ext2, ext3, acc, stage, came, sig1, sig2, base1, base2, tile, slots,
+    halo_send, halo_recv, relay_send, share_send, share_recv, part_send, part_recv, sum_send, sum_recv, load, store,
 ):
     pieces, devices, terms, blocks, width, entries = sizes
     share = width // pieces
@@ -40,6 +39,8 @@
     first = me_s * blocks - blocks
     has_low = me_s > 0
     has_high = me_s < devices - 1
+    odd = lax.rem(me_s, 2) == 1
+    even = jnp.logical_not(odd)
     zero = jnp.zeros((8, 128), F32)
 
     def device_at(offset):
@@ -52,6 +53,15 @@
     def rows_of(piece):
         return pl.ds(pl.multiple_of(piece * share, share), share)
 
+    half = blocks // 2
+    loads = [
+        pltpu.make_async_copy(source, target, load.at[i])
+        for i, (source, target) in enumerate(
+            ((left_in, left), (right_in, right), (pre_in, pre))
+        )
+    ]
+    for one in loads:
+        one.start()
     barrier = pltpu.get_barrier_semaphore()
 
     @pl.loop(1, count)
@@ -72,25 +82,80 @@
             device_id_type=MESH,
         )
 
-    def halo_start(ref, s, j, rows):
-        @pl.when(has_high)
+    def sends(j, s, relayed):
+        if j == 0:
+            return has_high, has_low
+        far = s < relayed
+        return (
+            has_high & jnp.logical_not(odd & far),
+            has_low & jnp.logical_not(even & far),
+        )
+
+    def halo_start(ref, s, j, relayed):
+        rows = rows_of(term_at(pieces - j))
+        up, down = sends(j, s, relayed)
+
+        @pl.when(up)
         def _():
             halo_copy(ref, s, j, True, rows).start()
 
-        @pl.when(has_low)
+        @pl.when(down)
         def _():
             halo_copy(ref, s, j, False, rows).start()
 
-    def halo_wait(ref, s, j, rows):
-        @pl.when(has_high)
-        def _():
-            halo_copy(ref, s, j, True, rows).wait_send()
-            halo_copy(ref, s, j, False, rows).wait_recv()
-
-        @pl.when(has_low)
-        def _():
-            halo_copy(ref, s, j, False, rows).wait_send()
-            halo_copy(ref, s, j, True, rows).wait_recv()
+    def relay_copy(ref, s, j, up):
+        slot = s if up else 2 * blocks + s
+        return pltpu.make_async_remote_copy(
+            src_ref=ref.at[slot, rows_of(me_t)],
+            dst_ref=ref.at[slot, rows_of(me_t)],
+            send_sem=relay_send.at[j - 1, s],
+            recv_sem=halo_recv.at[0 if up else 1, j, s],
+            device_id=(term_at(j), me_s),
+            device_id_type=MESH,
+        )
+
+    def relay(ref, s, relayed):
+        for up, here in ((True, has_low & even), (False, has_high & odd)):
+
+            @pl.when(here & (s < relayed))
+            def _():
+                halo_copy(ref, s, 0, up, rows_of(me_t)).wait_recv()
+                for j in range(1, pieces):
+                    relay_copy(ref, s, j, up).start()
+
+    def halo_wait(ref, s, relayed):
+        far = s < relayed
+        for j in range(pieces):
+            rows = rows_of(term_at(pieces - j))
+            up, down = sends(j, s, relayed)
+
+            @pl.when(up)
+            def _():
+                halo_copy(ref, s, j, True, rows).wait_send()
+
+            @pl.when(down)
+            def _():
+                halo_copy(ref, s, j, False, rows).wait_send()
+
+            low, high = has_low, has_high
+            if j == 0:
+                low = low & jnp.logical_not(even & far)
+                high = high & jnp.logical_not(odd & far)
+
+            @pl.when(low)
+            def _():
+                halo_copy(ref, s, j, True, rows).wait_recv()
+
+            @pl.when(high)
+            def _():
+                halo_copy(ref, s, j, False, rows).wait_recv()
+
+        for up, here in ((True, has_low & even), (False, has_high & odd)):
+
+            @pl.when(here & far)
+            def _():
+                for j in range(1, pieces):
+                    relay_copy(ref, s, j, up).wait_send()
 
     def share_copy(ref, s, offset, piece):
         return pltpu.make_async_remote_copy(
@@ -112,10 +177,13 @@
             device_id_type=MESH,
         )
 
+    lane = lax.broadcasted_iota(jnp.int32, (1, 128), 1)
+
     def sum_start(which, tiles):
-        rows = [jnp.sum(one, axis=0, keepdims=True) for one in tiles]
-        rows = rows + [jnp.zeros((1, 128), F32)] * (ROWS - len(rows))
-        packed = jnp.concatenate(rows, axis=0)
+        packed = jnp.zeros((1, 128), F32)
+        for i, one in enumerate(tiles):
+            row = jnp.sum(one, axis=0, keepdims=True)
+            packed = jnp.where(lane == i, jnp.sum(row, axis=1, keepdims=True), packed)
         tile[which] = packed
         slots[which, me] = packed
 
@@ -134,21 +202,18 @@
         others = slots.at[which, pl.ds(0, count - 1)]
         pltpu.make_async_copy(others, others, sum_recv.at[which]).wait()
         pltpu.make_async_copy(others, others, sum_send.at[which]).wait()
-        total = lax.fori_loop(
-            0, count, lambda i, t: t + slots[which, i], jnp.zeros((ROWS, 128), F32)
-        )
-        full = jnp.sum(total, axis=1, keepdims=True) / entries
-        return lambda row: full[row : row + 1, :]
+        full = jnp.sum(slots[which], axis=0) / entries
+        return lambda i: full[:, i : i + 1]
 
     row_ids = lax.broadcasted_iota(jnp.int32, (width, width), 0)
     col_ids = lax.broadcasted_iota(jnp.int32, (width, width), 1)
-    all_rows = pl.ds(0, width)
 
     @pl.loop(0, blocks)
     def _(s):
         keep = (row_ids < dims[0, s]) & (col_ids < dims[1, s])
         raw[blocks + s] = jnp.where(keep, psi[s].astype(F32), 0.0).astype(BF16)
-        halo_start(raw, s, 0, all_rows)
+        for j in range(pieces):
+            halo_start(raw, s, j, blocks)
 
     def chunk(i):
         return i // steps, pl.multiple_of(lax.rem(i, steps) * step, step)
@@ -162,6 +227,10 @@
         return total + fold(v * v)
 
     sum_start(0, [lax.fori_loop(0, blocks * steps, norm_step, zero)])
+    @pl.loop(0, blocks)
+    def _(s):
+        relay(raw, s, blocks)
+
     norm = sum_finish(0)(0)
     scale = 1.0 / jnp.sqrt(norm + epsilon)
 
@@ -175,7 +244,7 @@
 
     @pl.loop(0, blocks)
     def _(s):
-        halo_wait(raw, s, 0, all_rows)
+        halo_wait(raw, s, blocks)
 
         @pl.when(has_low)
         def _():
@@ -185,24 +254,20 @@
         def _():
             scaled(2 * blocks + s)
 
-    def product(ref, s, with_env):
+    def product(ref, s, keep):
         halves = []
         for t in range(terms):
             source = ref[jnp.clip(conn[t, s] - first, 0, 3 * blocks - 1)]
-            half = jnp.dot(left[t, s], source, preferred_element_type=F32).astype(BF16)
-            halves.append(half)
+            one = jnp.dot(left[t, s], source, preferred_element_type=F32).astype(BF16)
+            halves.append(one)
+            if keep:
+                env[t, s] = one
         total = None
         for t in range(terms):
             one = lax.dot_general(
                 halves[t], right[t, s], (((1,), (1,)), ((), ())), preferred_element_type=F32
             )
             total = one if total is None else total + one
-            if with_env:
-                new = lax.dot_general(
-                    ref[blocks + s], halves[t], (((0,), (0,)), ((), ())),
-                    preferred_element_type=F32,
-                )
-                env[t, s] = (new * width ** (-0.5)).astype(BF16)
         return total
 
     def apply(ref):
@@ -240,13 +305,14 @@
 
             for offset in range(1, pieces):
                 share_copy(ref, s, offset, me_t).start()
-            halo_start(ref, s, 0, rows_of(me_t))
+            halo_start(ref, s, 0, half)
 
         @pl.loop(0, blocks)
         def _(s):
             for offset in range(1, pieces):
                 share_copy(ref, s, offset, term_at(pieces - offset)).wait_recv()
-                halo_start(ref, s, offset, rows_of(term_at(pieces - offset)))
+                halo_start(ref, s, offset, half)
+            relay(ref, s, half)
 
         extra = meanwhile() if meanwhile is not None else None
 
@@ -254,10 +320,11 @@
         def _(s):
             for offset in range(1, pieces):
                 share_copy(ref, s, offset, me_t).wait_send()
-            for j in range(pieces):
-                halo_wait(ref, s, j, rows_of(term_at(pieces - j)))
+            halo_wait(ref, s, half)
         return extra
 
+    for one in loads:
+        one.wait()
     apply(ext1)
 
     def sums1(i, totals):
@@ -364,6 +431,20 @@
         return lax.fori_loop(0, width // step, inner, totals)
 
     sum_start(3, list(lax.fori_loop(0, blocks, sums3, (zero,) * 3)) + list(crossed))
+
+    def env_copy(t, s):
+        return pltpu.make_async_copy(env.at[t, s], env_out.at[t, s], store.at[t, s])
+
+    @pl.loop(0, blocks)
+    def _(s):
+        own = ext3[blocks + s]
+        for t in range(terms):
+            new = lax.dot_general(
+                own, env[t, s], (((0,), (0,)), ((), ())), preferred_element_type=F32
+            )
+            env[t, s] = (new * width ** (-0.5)).astype(BF16)
+            env_copy(t, s).start()
+
     end = sum_finish(3)
     cells = [
         [theta1, more(10), end(0)],
@@ -378,6 +459,11 @@
             out = jnp.where((row == i) & (col == j), cells[i][j], out)
     proj[...] = out
 
+    @pl.loop(0, blocks)
+    def _(s):
+        for t in range(terms):
+            env_copy(t, s).wait()
+
 
 def on_device(psi, left, right, connect, sector_dims, precond):
     blocks, width = psi.shape[0], psi.shape[1]
@@ -391,6 +477,7 @@
     dma = pltpu.SemaphoreType.DMA
     vmem = pl.BlockSpec(memory_space=pltpu.VMEM)
     smem = pl.BlockSpec(memory_space=pltpu.SMEM)
+    anywhere = pl.BlockSpec(memory_space=pl.ANY)
     proj, last, env = pl.pallas_call(
         functools.partial(kernel, sizes),
         name="davidson",
@@ -399,9 +486,13 @@
             jax.ShapeDtypeStruct((blocks, share, width), F32),
             jax.ShapeDtypeStruct((terms, blocks, width, width), BF16),
         ),
-        in_specs=[smem, smem, vmem, vmem, vmem, vmem],
-        out_specs=(vmem, vmem, vmem),
+        in_specs=[smem, smem, vmem, anywhere, anywhere, anywhere],
+        out_specs=(vmem, vmem, anywhere),
         scratch_shapes=[
+            pltpu.VMEM((terms, blocks, width, width), BF16),
+            pltpu.VMEM((terms, blocks, width, width), BF16),
+            pltpu.VMEM((blocks, width, width), BF16),
+            pltpu.VMEM((terms, blocks, width, width), BF16),
             pltpu.VMEM((3 * blocks, width, width), BF16),
             pltpu.VMEM((3 * blocks, width, width), BF16),
             pltpu.VMEM((3 * blocks, width, width), BF16),
@@ -413,16 +504,19 @@
             pltpu.VMEM((blocks, share, width), F32),
             pltpu.VMEM((blocks, share, width), F32),
             pltpu.VMEM((blocks, share, width), F32),
-            pltpu.VMEM((4, ROWS, 128), F32),
-            pltpu.VMEM((4, count, ROWS, 128), F32),
+            pltpu.VMEM((4, 1, 128), F32),
+            pltpu.VMEM((4, count, 1, 128), F32),
             dma((2, pieces, blocks)),
             dma((2, pieces, blocks)),
             dma((others, blocks)),
             dma((others, blocks)),
             dma((others, blocks)),
             dma((others, blocks)),
+            dma((others, blocks)),
             dma((4,)),
             dma((4,)),
+            dma((3,)),
+            dma((terms, blocks)),
         ],
         compiler_params=pltpu.CompilerParams(
             collective_id=0, has_side_effects=True, vmem_limit_bytes=60 * 1024 * 1024

time: 147 us -> 117 us (0.80)
  Pallas kernels: 139 us -> 109 us
    pallas_call x1, Pallas kernels: 139 us -> 109 us  [on_device(): pl.pallas_call(functools.partial(kernel, sizes), name='davidson', out_sha...]
where the time goes in v2:
time: 117 us
  Pallas kernels  109 us (93%)
  local copies, waits for them, and re-layouts  7.38 us (6%)
    pallas_call x1, Pallas kernels, on_device(): pl.pallas_call(functools.partial(kernel, sizes), name='davidson', out_sha...  109 us
    unnamed x2, local copies, waits for them, and re-layouts  6.12 us

profile of v2, /device:TPU:0, one launch (start us, length us, event | category | flops | bytes accessed | tf_op | source)
XLA Modules:
  0.0 116.6 jit_solution(15765363264855042676)
XLA Ops:
  0.6 108.6 %davidson.1 = (f32[8,128]{1,0:T(8,128)}, f32[8,128,256]{2,1,0:T(8,128)}, bf16[3,8,256,256]{3,2,1,0:T(8,128)(2,1)}) custom-call(s32[2,8]{1,0:T(2,128)} %dims.1, s32[3,8]{1,0:T(4,128)} %conn.1, bf16[8,256,256]{2,1,0:T(8,128)(2,1)} %psi.1, bf16[3,8,256,256]{3,2,1,0:T(8,128)(2,1)} %left_in.1, bf16[3,8,256,256]{3,2,1,0:T(8,128)(2,1)} %right_in.1, ...), custom_call_target="tpu_custom_call" | custom-call | tf_op jit(solution)/shard_map/davidson/pallas_call | solution.py:481
  109.2 1.3 %slice.3 = f32[3,3]{1,0:T(4,128)} slice(f32[8,128]{1,0:T(8,128)} %get-tuple-element.6), slice={[0:3], [0:3]} | slice | bytes 72 | tf_op jit(solution)/shard_map/slice | solution.py:525
  110.4 2.3 %copy.11 = f32[8,128,256]{2,1,0:T(8,128)} copy(f32[8,128,256]{2,1,0:T(8,128)} %get-tuple-element.13) | data formatting | bytes 2097152
  112.7 3.9 %copy.12 = bf16[3,8,256,256]{3,2,1,0:T(8,128)(2,1)} copy(bf16[3,8,256,256]{3,2,1,0:T(8,128)(2,1)} %get-tuple-element.14) | data formatting | bytes 6291456

commit v3 on v2

--- a/solution.py
+++ b/solution.py
@@ -23,9 +23,9 @@
 
 def kernel(
     sizes,
-    dims, conn, psi, left_in, right_in, pre_in,
-    proj, last, env_out,
-    left, right, pre, env, raw, ext1, ext2, ext3, acc, stage, came, sig1, sig2, base1, base2, tile, slots,
+    dims, conn, psi_in, left_in, right_in, pre_in,
+    proj, last_out, env_out,
+    left, right, pre, env, psi, last, inverse_of, raw, ext1, ext2, ext3, acc, stage, came, sig1, sig2, base1, base2, tile, slots,
     halo_send, halo_recv, relay_send, share_send, share_recv, part_send, part_recv, sum_send, sum_recv, load, store,
 ):
     pieces, devices, terms, blocks, width, entries = sizes
@@ -57,7 +57,7 @@
     loads = [
         pltpu.make_async_copy(source, target, load.at[i])
         for i, (source, target) in enumerate(
-            ((left_in, left), (right_in, right), (pre_in, pre))
+            ((psi_in, psi), (pre_in, pre), (left_in, left), (right_in, right))
         )
     ]
     for one in loads:
@@ -67,8 +67,6 @@
     @pl.loop(1, count)
     def _(offset):
         pl.semaphore_signal(barrier, inc=1, device_id=device_at(offset), device_id_type=MESH)
-
-    pl.semaphore_wait(barrier, count - 1)
 
     def halo_copy(ref, s, j, up, rows):
         slot = s if up else 2 * blocks + s
@@ -208,25 +206,39 @@
     row_ids = lax.broadcasted_iota(jnp.int32, (width, width), 0)
     col_ids = lax.broadcasted_iota(jnp.int32, (width, width), 1)
 
+    loads[0].wait()
+
     @pl.loop(0, blocks)
     def _(s):
         keep = (row_ids < dims[0, s]) & (col_ids < dims[1, s])
         raw[blocks + s] = jnp.where(keep, psi[s].astype(F32), 0.0).astype(BF16)
+
+    pl.semaphore_wait(barrier, count - 1)
+
+    @pl.loop(0, blocks)
+    def _(s):
         for j in range(pieces):
             halo_start(raw, s, j, blocks)
 
-    def chunk(i):
-        return i // steps, pl.multiple_of(lax.rem(i, steps) * step, step)
+    starts = [k * step for k in range(steps)]
 
     def own_rows(start):
         return pl.ds(pl.multiple_of(me_t * share + start, step), step)
 
-    def norm_step(i, total):
-        s, start = chunk(i)
-        v = raw[blocks + s, own_rows(start), :].astype(F32)
-        return total + fold(v * v)
-
-    sum_start(0, [lax.fori_loop(0, blocks * steps, norm_step, zero)])
+    def norm_step(s, total):
+        for start in starts:
+            v = raw[blocks + s, own_rows(start), :].astype(F32)
+            total = total + fold(v * v)
+        return total
+
+    sum_start(0, [lax.fori_loop(0, blocks, norm_step, zero)])
+    loads[1].wait()
+
+    @pl.loop(0, blocks)
+    def _(s):
+        for start in starts:
+            inverse_of[s, pl.ds(start, step), :] = 1.0 / pre[s, own_rows(start), :].astype(F32)
+
     @pl.loop(0, blocks)
     def _(s):
         relay(raw, s, blocks)
@@ -287,7 +299,7 @@
         return jnp.where((rows < dims[0, s]) & (cols < dims[1, s]), total, 0.0)
 
     def divided(s, start):
-        return 1.0 / pre[s, own_rows(start), :].astype(F32)
+        return inverse_of[s, pl.ds(start, step), :]
 
     def part_wait(s):
         for offset in range(1, pieces):
@@ -296,9 +308,7 @@
     def spread(ref, out, corr_of, meanwhile=None):
         @pl.loop(0, blocks)
         def _(s):
-            @pl.loop(0, steps)
-            def _(k):
-                start = pl.multiple_of(k * step, step)
+            for start in starts:
                 value = corr_of(s, start)
                 out[s, pl.ds(start, step), :] = value
                 ref[blocks + s, own_rows(start), :] = value.astype(BF16)
@@ -323,18 +333,18 @@
             halo_wait(ref, s, half)
         return extra
 
-    for one in loads:
-        one.wait()
+    loads[2].wait()
+    loads[3].wait()
     apply(ext1)
 
-    def sums1(i, totals):
-        s, start = chunk(i)
+    def sums1(s, totals):
+        part_wait(s)
+        for start in starts:
+            totals = sums1_rows(s, start, totals)
+        return totals
+
+    def sums1_rows(s, start, totals):
         here = pl.ds(start, step)
-
-        @pl.when(start == 0)
-        def _():
-            part_wait(s)
-
         sigma = masked_sum(s, start)
         sig1[s, here, :] = sigma
         inverse = divided(s, start)
@@ -344,7 +354,7 @@
         pairs = [(b1, sigma), (b1, r), (b1, q), (r, r), (r, q), (q, q), (b1, b1)]
         return tuple(t + fold(x * y) for t, (x, y) in zip(totals, pairs))
 
-    sum_start(1, lax.fori_loop(0, blocks * steps, sums1, (zero,) * 7))
+    sum_start(1, lax.fori_loop(0, blocks, sums1, (zero,) * 7))
     got = sum_finish(1)
     theta1 = got(0)
     first_gram = got(6)
@@ -366,14 +376,14 @@
 
     apply(ext2)
 
-    def sums2(i, totals):
-        s, start = chunk(i)
+    def sums2(s, totals):
+        part_wait(s)
+        for start in starts:
+            totals = sums2_rows(s, start, totals)
+        return totals
+
+    def sums2_rows(s, start, totals):
         here = pl.ds(start, step)
-
-        @pl.when(start == 0)
-        def _():
-            part_wait(s)
-
         sigma = masked_sum(s, start)
         sig2[s, here, :] = sigma
         inverse = divided(s, start)
@@ -387,7 +397,7 @@
         ]
         return tuple(t + fold(x * y) for t, (x, y) in zip(totals, pairs))
 
-    sum_start(2, lax.fori_loop(0, blocks * steps, sums2, (zero,) * 12))
+    sum_start(2, lax.fori_loop(0, blocks, sums2, (zero,) * 12))
     more = sum_finish(2)
     theta2 = more(0)
     weight1 = more(1) - theta2 * more(3)
@@ -408,27 +418,31 @@
         corr = (sig2[s, here, :] - theta2 * b2) * divided(s, start)
         return (corr - weight1 * b1 - weight2 * b2) * scale2
 
-    def cross(i, totals):
-        s, start = chunk(i)
-        here = pl.ds(start, step)
-        b3 = last[s, here, :]
-        pairs = [(b3, sig1[s, here, :]), (b3, sig2[s, here, :])]
-        return tuple(t + fold(x * y) for t, (x, y) in zip(totals, pairs))
-
-    crossed = spread(
-        ext3, last, corr2, lambda: lax.fori_loop(0, blocks * steps, cross, (zero,) * 2)
-    )
+    def cross(s, totals):
+        for start in starts:
+            here = pl.ds(start, step)
+            b3 = last[s, here, :]
+            pairs = [(b3, sig1[s, here, :]), (b3, sig2[s, here, :])]
+            totals = tuple(t + fold(x * y) for t, (x, y) in zip(totals, pairs))
+        return totals
+
+    last_copy = pltpu.make_async_copy(last, last_out, load.at[0])
+
+    def meanwhile():
+        last_copy.start()
+        return lax.fori_loop(0, blocks, cross, (zero,) * 2)
+
+    crossed = spread(ext3, last, corr2, meanwhile)
 
     def sums3(s, totals):
         acc[s] = product(ext3, s, True)
 
-        def inner(k, totals):
-            here = pl.ds(pl.multiple_of(k * step, step), step)
+        for start in range(0, width, step):
+            here = pl.ds(start, step)
             sigma = acc[s, here, :]
             vectors = [ref[blocks + s, here, :].astype(F32) for ref in (ext1, ext2, ext3)]
-            return tuple(t + fold(v * sigma) for t, v in zip(totals, vectors))
-
-        return lax.fori_loop(0, width // step, inner, totals)
+            totals = tuple(t + fold(v * sigma) for t, v in zip(totals, vectors))
+        return totals
 
     sum_start(3, list(lax.fori_loop(0, blocks, sums3, (zero,) * 3)) + list(crossed))
 
@@ -463,6 +477,8 @@
     def _(s):
         for t in range(terms):
             env_copy(t, s).wait()
+
+    last_copy.wait()
 
 
 def on_device(psi, left, right, connect, sector_dims, precond):
@@ -486,13 +502,16 @@
             jax.ShapeDtypeStruct((blocks, share, width), F32),
             jax.ShapeDtypeStruct((terms, blocks, width, width), BF16),
         ),
-        in_specs=[smem, smem, vmem, anywhere, anywhere, anywhere],
-        out_specs=(vmem, vmem, anywhere),
+        in_specs=[smem, smem, anywhere, anywhere, anywhere, anywhere],
+        out_specs=(vmem, anywhere, anywhere),
         scratch_shapes=[
             pltpu.VMEM((terms, blocks, width, width), BF16),
             pltpu.VMEM((terms, blocks, width, width), BF16),
             pltpu.VMEM((blocks, width, width), BF16),
             pltpu.VMEM((terms, blocks, width, width), BF16),
+            pltpu.VMEM((blocks, width, width), BF16),
+            pltpu.VMEM((blocks, share, width), F32),
+            pltpu.VMEM((blocks, share, width), F32),
             pltpu.VMEM((3 * blocks, width, width), BF16),
             pltpu.VMEM((3 * blocks, width, width), BF16),
             pltpu.VMEM((3 * blocks, width, width), BF16),
@@ -515,7 +534,7 @@
             dma((others, blocks)),
             dma((4,)),
             dma((4,)),
-            dma((3,)),
+            dma((4,)),
             dma((terms, blocks)),
         ],
         compiler_params=pltpu.CompilerParams(

time: 117 us -> 114 us (0.974)
  Pallas kernels: 109 us -> 106 us
    pallas_call x1, Pallas kernels: 109 us -> 106 us  [on_device(): pl.pallas_call(functools.partial(kernel, sizes), name='davidson', out_sha...]
where the time goes in v3:
time: 114 us
  Pallas kernels  106 us (93%)
  local copies, waits for them, and re-layouts  7.38 us (6%)
    pallas_call x1, Pallas kernels, on_device(): pl.pallas_call(functools.partial(kernel, sizes), name='davidson', out_sha...  106 us
    unnamed x2, local copies, waits for them, and re-layouts  6.12 us

profile of v3, /device:TPU:0, one launch (start us, length us, event | category | flops | bytes accessed | tf_op | source)
XLA Modules:
  0.0 113.9 jit_solution(10101007733445518850)
XLA Ops:
  0.6 105.9 %davidson.1 = (f32[8,128]{1,0:T(8,128)}, f32[8,128,256]{2,1,0:T(8,128)}, bf16[3,8,256,256]{3,2,1,0:T(8,128)(2,1)}) custom-call(s32[2,8]{1,0:T(2,128)} %dims.1, s32[3,8]{1,0:T(4,128)} %conn.1, bf16[8,256,256]{2,1,0:T(8,128)(2,1)} %psi_in.1, bf16[3,8,256,256]{3,2,1,0:T(8,128)(2,1)} %left_in.1, bf16[3,8,256,256]{3,2,1,0:T(8,128)(2,1)} %right_in.1, ...), custom_call_target="tpu_custom_call" | custom-call | tf_op jit(solution)/shard_map/davidson/pallas_call | solution.py:497
  106.5 1.3 %slice.3 = f32[3,3]{1,0:T(4,128)} slice(f32[8,128]{1,0:T(8,128)} %get-tuple-element.6), slice={[0:3], [0:3]} | slice | bytes 72 | tf_op jit(solution)/shard_map/slice | solution.py:544
  107.8 2.3 %copy.11 = f32[8,128,256]{2,1,0:T(8,128)} copy(f32[8,128,256]{2,1,0:T(8,128)} %get-tuple-element.13) | data formatting | bytes 2097152
  110.0 3.9 %copy.12 = bf16[3,8,256,256]{3,2,1,0:T(8,128)(2,1)} copy(bf16[3,8,256,256]{3,2,1,0:T(8,128)(2,1)} %get-tuple-element.14) | data formatting | bytes 6291456

commit v4 on v3

--- a/solution.py
+++ b/solution.py
@@ -199,7 +199,6 @@
     def sum_finish(which):
         others = slots.at[which, pl.ds(0, count - 1)]
         pltpu.make_async_copy(others, others, sum_recv.at[which]).wait()
-        pltpu.make_async_copy(others, others, sum_send.at[which]).wait()
         full = jnp.sum(slots[which], axis=0) / entries
         return lambda i: full[:, i : i + 1]
 
@@ -479,6 +478,9 @@
             env_copy(t, s).wait()
 
     last_copy.wait()
+    for which in range(4):
+        others = slots.at[which, pl.ds(0, count - 1)]
+        pltpu.make_async_copy(others, others, sum_send.at[which]).wait()
 
 
 def on_device(psi, left, right, connect, sector_dims, precond):

time: 114 us -> 114 us (level)
  no operation moved by 1% of the time
where the time goes in v4:
time: 114 us
  Pallas kernels  106 us (93%)
  local copies, waits for them, and re-layouts  7.38 us (6%)
    pallas_call x1, Pallas kernels, on_device(): pl.pallas_call(functools.partial(kernel, sizes), name='davidson', out_sha...  106 us
    unnamed x2, local copies, waits for them, and re-layouts  6.12 us

profile of v4, /device:TPU:0, one launch (start us, length us, event | category | flops | bytes accessed | tf_op | source)
XLA Modules:
  0.0 113.9 jit_solution(13971526279526680476)
XLA Ops:
  0.6 105.9 %davidson.1 = (f32[8,128]{1,0:T(8,128)}, f32[8,128,256]{2,1,0:T(8,128)}, bf16[3,8,256,256]{3,2,1,0:T(8,128)(2,1)}) custom-call(s32[2,8]{1,0:T(2,128)} %dims.1, s32[3,8]{1,0:T(4,128)} %conn.1, bf16[8,256,256]{2,1,0:T(8,128)(2,1)} %psi_in.1, bf16[3,8,256,256]{3,2,1,0:T(8,128)(2,1)} %left_in.1, bf16[3,8,256,256]{3,2,1,0:T(8,128)(2,1)} %right_in.1, ...), custom_call_target="tpu_custom_call" | custom-call | tf_op jit(solution)/shard_map/davidson/pallas_call | solution.py:499
  106.5 1.3 %slice.3 = f32[3,3]{1,0:T(4,128)} slice(f32[8,128]{1,0:T(8,128)} %get-tuple-element.6), slice={[0:3], [0:3]} | slice | bytes 72 | tf_op jit(solution)/shard_map/slice | solution.py:546
  107.8 2.3 %copy.11 = f32[8,128,256]{2,1,0:T(8,128)} copy(f32[8,128,256]{2,1,0:T(8,128)} %get-tuple-element.13) | data formatting | bytes 2097152
  110.0 3.9 %copy.12 = bf16[3,8,256,256]{3,2,1,0:T(8,128)(2,1)} copy(bf16[3,8,256,256]{3,2,1,0:T(8,128)(2,1)} %get-tuple-element.14) | data formatting | bytes 6291456
